TPU v7x, 32 devices: a whole 2x2x4 slice. The times are simulated.
32 devices in a mesh: rows: 8 (over y, x, core), cols: 4 (over z).
Axes of the slice: x: 2, y: 2, z: 4, core: 2. Of those that a mesh axis runs over, the one named last changes fastest.
Arguments:
- grads: bfloat16 [9216, 8192], P(('rows', 'cols')), may hold values from -6 to 6
- tests: float32 [64, 8192], P(None, 'cols'), may hold values from -6 to 6
Outputs:
- solution: float32 [64, 8192], P(None, 'cols')
- scores: float32 [64, 9216], P(None, ('rows', 'cols'))
All inputs are finite; a program needn't handle non-finite values.
Results may differ from a plain program's by a relative error of at most 0.0041.
Values may be sent and summed in bfloat16 or wider, within the bound.
A program may use at most 64 MiB of HBM per device.

v0:
```python
import jax
import jax.numpy as jnp
from jax import lax
from jax.sharding import PartitionSpec as P

damping = 0.5


def per_device(grads, tests):
    n_total = grads.shape[0] * lax.axis_size("rows") * lax.axis_size("cols")
    width = grads.shape[1]
    own = tests.shape[1]
    direction = lax.all_gather(tests, "cols", axis=1, tiled=True)
    norm_now = jnp.sum(direction * direction, axis=1)

    def project(d):
        return lax.dot_general(
            grads,
            d.astype(jnp.bfloat16),
            (((1,), (1,)), ((), ())),
            preferred_element_type=jnp.float32,
        )

    partial_value = lax.dot_general(
        project(direction).astype(jnp.bfloat16),
        grads,
        (((0,), (0,)), ((), ())),
        preferred_element_type=jnp.float32,
    )
    image = lax.psum(partial_value, ("rows", "cols")) / n_total + damping * direction
    alpha = norm_now / jnp.sum(direction * image, axis=1)
    solution = alpha[:, None] * direction
    residual = direction - alpha[:, None] * image
    norm_next = jnp.sum(residual * residual, axis=1)
    direction = residual + (norm_next / norm_now)[:, None] * direction
    proj = project(direction)
    curv = lax.psum(
        jnp.sum(proj * proj.astype(jnp.bfloat16).astype(jnp.float32), axis=0), ("rows", "cols")
    )
    curv = curv / n_total + damping * jnp.sum(direction * direction, axis=1)
    solution = solution + (norm_next / curv)[:, None] * direction
    scores = lax.dot_general(
        solution.astype(jnp.bfloat16),
        grads,
        (((1,), (1,)), ((), ())),
        preferred_element_type=jnp.float32,
    )
    mine = lax.dynamic_slice_in_dim(solution, lax.axis_index("cols") * own, own, axis=1)
    return (mine, scores * width ** (-0.5))


def solution(mesh):
    placed = (P(("rows", "cols"), None), P(None, "cols"))
    return jax.shard_map(
        per_device,
        mesh=mesh,
        in_specs=placed,
        out_specs=(P(None, "cols"), P(None, ("rows", "cols"))),
        check_vma=False,
    )
```

profile of v0, /device:TPU:0, one launch (start us, length us, event | category | flops | bytes accessed | tf_op | source)
XLA Modules:
  0.0 261.7 jit_solution(16199284651384448593)
XLA Ops:
  7.2 0.0 all-gather.2.cloned.1.call-start
  7.2 0.7 all-gather.2.cloned.1.call-update
  7.9 0.0 all-reduce.2.cloned.1.call-start
  7.9 50.0 %all-gather.2.cloned.1.call-done = f32[64,8192]{1,0:T(8,128)} async-done(((f32[64,2048]{1,0:T(8,128)}), f32[64,8192]{1,0:T(8,128)}) %all-gather.2.cloned.1.call-update) | async-done | bytes 2097168 | tf_op jit(solution)/shard_map/all_gather | solution.py:13
  58.0 9.7 %fusion = f32[64,8192]{1,0:T(8,128)} fusion(bf16[288,8192]{1,0:T(8,128)(2,1)} %param.2, f32[64,8192]{1,0:T(8,128)} %all-gather.2.cloned.1.call-done), kind=kOutput, calls=%fused_computation.11 | convolution fusion | flops 604522496 | bytes 8912896 | tf_op jit(solution)/shard_map/dot_general | solution.py:24
  67.6 0.0 copy-start
  67.6 0.0 all-reduce.2.cloned.1.call-update
  67.7 133.7 %all-reduce.2.cloned.1.call-done = f32[64,8192]{1,0:T(8,128)} async-done(((f32[64,8192]{1,0:T(8,128)}), f32[64,8192]{1,0:T(8,128)}) %all-reduce.2.cloned.1.call-update) | async-done | bytes 2097168 | tf_op jit(solution)/shard_map/psum | solution.py:30
  201.4 0.0 copy-done
  201.4 0.0 copy-start.1
  201.4 2.3 multiply_reduce_fusion.2
  203.7 0.0 copy-start.2
  203.7 2.3 multiply_reduce_fusion.1
  206.1 0.0 copy-done.1
  206.1 0.0 copy-done.2
  206.1 0.0 slice-start
  206.1 1.8 multiply_reduce_fusion.4
  207.9 38.9 %psum.15 = f32[64]{0:T(128)S(1)} all-reduce(f32[64]{0:T(128)S(1)} %multiply_reduce_fusion.4), channel_id=1, replica_groups=mesh['rows'=8,'cols'=4] {'rows','cols'}, use_global_device_ids=true, to_apply=%region_5.0 | all-reduce | flops 64 | bytes 512 | tf_op jit(solution)/shard_map/psum | solution.py:37
  246.9 2.5 multiply_reduce_fusion
  249.4 2.3 multiply_add_fusion
  251.7 0.0 slice-done
  251.7 0.0 slice-done.1
  251.7 2.3 convolution_multiply_fusion
  254.0 0.8 constant_dynamic-slice_fusion
  (5 shorter events, 0.0 us)
Async XLA Ops:
  7.2 50.8 %all-gather.2.cloned.1.call-start = ((), (), s32[]{:S(2)}) async-start(), calls=%async_computation | async-start | bytes 2621440 | tf_op jit(solution)/shard_map/all_gather | solution.py:13
  7.9 193.5 %all-reduce.2.cloned.1.call-start = ((), (), s32[]{:S(2)}) async-start(), calls=%async_computation.1 | async-start | bytes 4194304 | tf_op jit(solution)/shard_map/psum | solution.py:30
  67.6 133.7 %copy-start = (f32[64,8192]{1,0:T(8,128)S(1)}, f32[64,8192]{1,0:T(8,128)}, u32[]{:S(2)}) copy-start(f32[64,8192]{1,0:T(8,128)} %all-gather.2.cloned.1.call-done) | copy-start | bytes 6291460
  201.4 4.7 %copy-start.1 = (bf16[288,8192]{1,0:T(8,128)(2,1)S(1)}, bf16[288,8192]{1,0:T(8,128)(2,1)}, u32[]{:S(2)}) copy-start(bf16[288,8192]{1,0:T(8,128)(2,1)} %param.2) | copy-start | bytes 14155780
  203.7 2.4 copy-start.2
  206.1 45.6 %slice-start = ((s8[4718592]{0:T(1024)(128)(4,1)}), s8[524288]{0:T(1024)(128)(4,1)S(1)}, s32[]{:S(2)}) async-start(s8[4718592]{0:T(1024)(128)(4,1)} %bitcast.8), calls=%async_computation.2 | async-start | bytes 1048576
  246.9 4.8 %slice-start.1 = ((s8[4718592]{0:T(1024)(128)(4,1)}), s8[4194304]{0:T(1024)(128)(4,1)S(1)}, s32[]{:S(2)}) async-start(s8[4718592]{0:T(1024)(128)(4,1)} %bitcast.8), calls=%async_computation.3 | async-start | bytes 8388608
Sparse Core Ops, SparseCore 0:
  9.5 48.3 all-gather.1
  67.8 133.5 all-reduce.1
where the time goes:
time: 262 us
  waiting for transfers between devices  184 us (70%)
  blocking collectives  38.9 us (15%)
  between operations  14.1 us (5%)
  matrix products  13.8 us (5%)
  other arithmetic  9.47 us (4%)
    psum x1, waiting for transfers between devices, per_device(): lax.psum(partial_value, ('rows', 'cols')) / n_total + damping * direction  134 us
    all_gather x1, waiting for transfers between devices, per_device(): direction = lax.all_gather(tests, 'cols', axis=1, tiled=True)  50 us
    psum x1, blocking collectives, per_device(): lax.psum(jnp.sum(proj * proj.astype(jnp.bfloat16).astype(jnp.float32), ax...  38.9 us
    dot_general x1, matrix products, per_device(): lax.dot_general(project(direction).astype(jnp.bfloat16), grads, (((0,), (...  9.67 us
  transfers between devices with their start and end apart: 2, of which 2 were waited for; matrix products, arithmetic and copies ran while one was open for 0% of the time, Pallas kernels for 0%

commit v1 on v0

--- a/solution.py
+++ b/solution.py
@@ -6,11 +6,43 @@
 damping = 0.5
 
 
+def do_samples(matrix):
+    now = lax.psum(1, "cols")
+    x_new, u_next, t1 = (now, lax.axis_index("cols"), matrix.shape[1])
+    inbox = []
+    q = 0
+    while q < x_new:
+        inbox.append((q, (q + 1) % x_new))
+        q += 1
+    row_list = []
+    q = 0
+    while q < x_new:
+        row_list.append((q, (q - 1) % x_new))
+        q = q + 1
+    mixed_arr = jnp.zeros((*matrix.shape[:1], x_new * t1, *matrix.shape[2:]), matrix.dtype)
+    mixed_arr = lax.dynamic_update_slice_in_dim(mixed_arr, matrix, u_next * t1, axis=1)
+    tall = newest = matrix
+    y1 = x_new // 2
+    kk = 1
+    while kk < y1 + 1:
+        tall = lax.ppermute(tall, "cols", inbox)
+        mixed_arr = lax.dynamic_update_slice_in_dim(
+            mixed_arr, tall, (u_next - kk) % x_new * t1, axis=1
+        )
+        if kk < x_new - y1:
+            newest = lax.ppermute(newest, "cols", row_list)
+            mixed_arr = lax.dynamic_update_slice_in_dim(
+                mixed_arr, newest, (u_next + kk) % x_new * t1, axis=1
+            )
+        kk = kk + 1
+    return mixed_arr
+
+
 def per_device(grads, tests):
     n_total = grads.shape[0] * lax.axis_size("rows") * lax.axis_size("cols")
     width = grads.shape[1]
     own = tests.shape[1]
-    direction = lax.all_gather(tests, "cols", axis=1, tiled=True)
+    direction = do_samples(tests)
     norm_now = jnp.sum(direction * direction, axis=1)
 
     def project(d):

time: 262 us -> 253 us (0.966)
  waiting for transfers between devices: 184 us -> 167 us
  starting transfers between devices: 0.08 us -> 5.24 us
    all_gather x1 -> x0, waiting for transfers between devices: 50 us -> none  [per_device(): direction = lax.all_gather(tests, 'cols', axis=1, tiled=True)]
    ppermute x0 -> x3, waiting for transfers between devices: none -> 33.3 us  [the longest x2 23.5 us: do_samples(): tall = lax.ppermute(tall, 'cols', inbox)]
    ppermute x0 -> x3, starting transfers between devices: none -> 5.2 us  [the longest x2 3.11 us: do_samples(): tall = lax.ppermute(tall, 'cols', inbox)]
  transfers between devices with their start and end apart: 2 -> 4, of which waited for: 2 -> 4; matrix products, arithmetic and copies ran while one was open for 0% -> 1% of each run, Pallas kernels for 0% -> 0%
where the time goes in v1:
time: 253 us
  waiting for transfers between devices  167 us (66%)
  blocking collectives  39 us (15%)
  matrix products  15.7 us (6%)
  between operations  14.2 us (6%)
  other arithmetic  7.81 us (3%)
  starting transfers between devices  5.24 us (2%)
  local copies, waits for them, and re-layouts  3.22 us (1%)
    psum x1, waiting for transfers between devices, per_device(): lax.psum(partial_value, ('rows', 'cols')) / n_total + damping * direction  134 us
    psum x1, blocking collectives, per_device(): lax.psum(jnp.sum(proj * proj.astype(jnp.bfloat16).astype(jnp.float32), ax...  39 us
    ppermute x2, waiting for transfers between devices, do_samples(): tall = lax.ppermute(tall, 'cols', inbox)  23.5 us
    ppermute x1, waiting for transfers between devices, do_samples(): newest = lax.ppermute(newest, 'cols', row_list)  9.81 us
    dot_general x1, matrix products, per_device(): lax.dot_general(project(direction).astype(jnp.bfloat16), grads, (((0,), (...  9.23 us
  transfers between devices with their start and end apart: 4, of which 4 were waited for; matrix products, arithmetic and copies ran while one was open for 1% of the time, Pallas kernels for 0%

profile of v1, /device:TPU:0, one launch (start us, length us, event | category | flops | bytes accessed | tf_op | source)
XLA Modules:
  0.0 252.5 jit_solution(15144454892165701603)
XLA Ops:
  7.2 0.0 copy-start.1
  7.2 0.0 all-reduce.2.cloned.1.call-start
  7.2 3.1 %collective-permute-start = (f32[64,2048]{1,0:T(8,128)}, f32[64,2048]{1,0:T(8,128)S(1)}, u32[]{:S(2)}, u32[]{:S(2)}) collective-permute-start(f32[64,2048]{1,0:T(8,128)} %param.3), channel_id=1, source_target_pairs={{0,1},{1,2},{2,3},{3,0},{4,5},{5,6},{6,7},{7,4},{8,9},{9,10},{10,1... | collective-permute-start | bytes 1572872 | tf_op jit(solution)/shard_map/ppermute | solution.py:28
  10.3 2.1 collective-permute-start.1
  12.4 13.0 %collective-permute-done = f32[64,2048]{1,0:T(8,128)S(1)} collective-permute-done((f32[64,2048]{1,0:T(8,128)}, f32[64,2048]{1,0:T(8,128)S(1)}, u32[]{:S(2)}, u32[]{:S(2)}) %collective-permute-start) | collective-permute-done | bytes 524320 | tf_op jit(solution)/shard_map/ppermute | solution.py:28
  25.4 0.0 collective-permute-start.2
  25.4 0.1 broadcast_in_dim.2
  25.5 0.0 copy-done.1
  25.7 9.8 %collective-permute-done.1 = f32[64,2048]{1,0:T(8,128)} collective-permute-done((f32[64,2048]{1,0:T(8,128)}, f32[64,2048]{1,0:T(8,128)}, u32[]{:S(2)}, u32[]{:S(2)}) %collective-permute-start.1) | collective-permute-done | bytes 524320 | tf_op jit(solution)/shard_map/ppermute | solution.py:33
  35.5 1.1 constant_dynamic-update-slice_fusion.1
  36.6 10.5 %collective-permute-done.2 = f32[64,2048]{1,0:T(8,128)} collective-permute-done((f32[64,2048]{1,0:T(8,128)S(1)}, f32[64,2048]{1,0:T(8,128)}, u32[]{:S(2)}, u32[]{:S(2)}) %collective-permute-start.2) | collective-permute-done | bytes 524320 | tf_op jit(solution)/shard_map/ppermute | solution.py:28
  47.1 1.1 constant_dynamic-update-slice_fusion
  48.2 9.2 %fusion = f32[64,8192]{1,0:T(8,128)} fusion(bf16[288,8192]{1,0:T(8,128)(2,1)} %param.2, f32[64,8192]{1,0:T(8,128)S(1)} %constant_dynamic-update-slice_fusion), kind=kOutput, calls=%fused_computation.11 | convolution fusion | flops 604522496 | bytes 8912896 | tf_op jit(solution)/shard_map/dot_general | solution.py:56
  57.4 0.0 all-reduce.2.cloned.1.call-update
  57.4 134.0 %all-reduce.2.cloned.1.call-done = f32[64,8192]{1,0:T(8,128)} async-done(((f32[64,8192]{1,0:T(8,128)}), f32[64,8192]{1,0:T(8,128)}) %all-reduce.2.cloned.1.call-update) | async-done | bytes 2097168 | tf_op jit(solution)/shard_map/psum | solution.py:62
  191.5 2.3 multiply_reduce_fusion.2
  193.8 0.7 multiply_reduce_fusion.1
  194.5 0.0 slice-start
  194.5 4.2 %multiply_reduce_fusion.4 = f32[64]{0:T(128)S(1)} fusion(bf16[288,8192]{1,0:T(8,128)(2,1)} %param.2, f32[64,8192]{1,0:T(8,128)S(1)} %constant_dynamic-update-slice_fusion, f32[64,8192]{1,0:T(8,128)S(1)} %copy-done, f32[64]{0:T(128)S(1)} %div.32, f32[64]{0:T(128)S(1)} %div.31), kind=kOutput, calls=%fused_computation.15 | convolution fusion | flops 306257856 | bytes 8913664 | tf_op jit(solution)/shard_map/dot_general | solution.py:49
  198.7 39.0 %psum.15 = f32[64]{0:T(128)S(1)} all-reduce(f32[64]{0:T(128)S(1)} %multiply_reduce_fusion.4), channel_id=1, replica_groups=mesh['rows'=8,'cols'=4] {'rows','cols'}, use_global_device_ids=true, to_apply=%region_5.6 | all-reduce | flops 64 | bytes 512 | tf_op jit(solution)/shard_map/psum | solution.py:69
  237.7 2.5 multiply_reduce_fusion
  240.2 2.3 multiply_add_fusion
  242.6 2.3 convolution_multiply_fusion
  244.8 0.8 constant_dynamic-slice_fusion
  (11 shorter events, 0.1 us)
Async XLA Ops:
  7.2 18.4 %copy-start.1 = (f32[64,2048]{1,0:T(8,128)S(1)}, f32[64,2048]{1,0:T(8,128)}, u32[]{:S(2)}) copy-start(f32[64,2048]{1,0:T(8,128)} %param.3) | copy-start | bytes 1572868
  7.2 184.3 %all-reduce.2.cloned.1.call-start = ((), (), s32[]{:S(2)}) async-start(), calls=%async_computation | async-start | bytes 4194304 | tf_op jit(solution)/shard_map/psum | solution.py:62
  7.2 18.2 %collective-permute-start = (f32[64,2048]{1,0:T(8,128)}, f32[64,2048]{1,0:T(8,128)S(1)}, u32[]{:S(2)}, u32[]{:S(2)}) collective-permute-start(f32[64,2048]{1,0:T(8,128)} %param.3), channel_id=1, source_target_pairs={{0,1},{1,2},{2,3},{3,0},{4,5},{5,6},{6,7},{7,4},{8,9},{9,10},{10,1... | collective-permute-start | bytes 1572872 | tf_op jit(solution)/shard_map/ppermute | solution.py:28
  10.3 25.2 %collective-permute-start.1 = (f32[64,2048]{1,0:T(8,128)}, f32[64,2048]{1,0:T(8,128)}, u32[]{:S(2)}, u32[]{:S(2)}) collective-permute-start(f32[64,2048]{1,0:T(8,128)} %param.3), channel_id=1, source_target_pairs={{0,3},{1,0},{2,1},{3,2},{4,7},{5,4},{6,5},{7,6},{8,11},{9,8},{10,9... | collective-permute-start | bytes 1572872 | tf_op jit(solution)/shard_map/ppermute | solution.py:33
  25.4 21.7 %collective-permute-start.2 = (f32[64,2048]{1,0:T(8,128)S(1)}, f32[64,2048]{1,0:T(8,128)}, u32[]{:S(2)}, u32[]{:S(2)}) collective-permute-start(f32[64,2048]{1,0:T(8,128)S(1)} %collective-permute-done), channel_id=1, source_target_pairs={{0,1},{1,2},{2,3},{3,0},{4,5},{5,6},{6,7},{7,4},{8,9},{9,10},{10,1... | collective-permute-start | bytes 1572872 | tf_op jit(solution)/shard_map/ppermute | solution.py:28
  191.5 2.3 copy-start
  194.5 48.0 %slice-start = ((s8[4718592]{0:T(1024)(128)(4,1)}), s8[524288]{0:T(1024)(128)(4,1)S(1)}, s32[]{:S(2)}) async-start(s8[4718592]{0:T(1024)(128)(4,1)} %bitcast.8), calls=%async_computation.1 | async-start | bytes 1048576
  237.7 4.8 %slice-start.1 = ((s8[4718592]{0:T(1024)(128)(4,1)}), s8[4194304]{0:T(1024)(128)(4,1)S(1)}, s32[]{:S(2)}) async-start(s8[4718592]{0:T(1024)(128)(4,1)} %bitcast.8), calls=%async_computation.2 | async-start | bytes 8388608
Sparse Core Ops, SparseCore 0:
  57.6 133.8 all-reduce.1
